TPU v7x, 32 devices: a whole 2x2x4 slice. The times are simulated.
32 devices in a mesh: gx: 4 (over y, x), gy: 8 (over z, core).
Axes of the slice: x: 2, y: 2, z: 4, core: 2. Of those that a mesh axis runs over, the one named last changes fastest.
Arguments:
- inputs: bfloat16 [16, 16, 32, 512], P('gx', 'gy'), may hold values from -6 to 6
- cotangent: bfloat16 [16, 16, 32, 512], P('gx', 'gy'), may hold values from -6 to 6
- point_weight: bfloat16 [32, 32], replicated, may hold values from -1 to 1
- spectral_weight: bfloat16 [2304, 24, 2048], P(('gx', 'gy')), may hold values from -0.75 to 0.75
Outputs:
- grad_input: bfloat16 [16, 16, 32, 512], P('gx', 'gy')
- grad_spectral: float32 [2304, 24, 2048], P(('gx', 'gy'))
All inputs are finite; a program needn't handle non-finite values.
Results may differ from a plain program's by a relative error of at most 0.034.
Values may be sent and summed in bfloat16 or wider, within the bound.
No kernel may reach another device: no remote copies, remote signals or barrier semaphores. Data moves between devices by JAX's collectives and lax.ppermute only.
A program may use at most 192 MiB of HBM per device.

v0:
```python
import math
import jax
import jax.numpy as jnp
from jax import lax
from jax.sharding import PartitionSpec as P

NZ = 64
NT = 8
KX = 24
KY = 24
KZ = 12
KT = 8


def kept_angles(positions, kept_count, length):
    index = jnp.arange(kept_count, dtype=jnp.int32)
    frequency = jnp.where(index < kept_count // 2, index, index - kept_count)
    turns = positions[:, None] * frequency[None, :] % length
    return turns.astype(jnp.float32) * (2.0 * math.pi / length)


def axis_tables(positions, kept_count, length):
    angles = kept_angles(positions, kept_count, length)
    return (jnp.cos(angles), jnp.sin(angles))


def depth_tables():
    angle_depth = kept_angles(jnp.arange(NZ, dtype=jnp.int32), KZ, NZ)
    angle_time = kept_angles(jnp.arange(NT, dtype=jnp.int32), KT, NT)
    angles = (angle_depth[:, None, :, None] + angle_time[None, :, None, :]).reshape(
        NZ * NT, KZ * KT
    )
    return (jnp.cos(angles), jnp.sin(angles))


def settle(values):
    return lax.optimization_barrier(values.astype(jnp.bfloat16))


def rotate(spectra, cosine_table, sine_table, pattern, turn_sign):
    half_width = spectra.shape[-1] // 2
    with_cosine = jnp.einsum(pattern, spectra, cosine_table, precision=lax.Precision.HIGHEST)
    with_sine = jnp.einsum(pattern, spectra, sine_table, precision=lax.Precision.HIGHEST)
    real_part = with_cosine[..., :half_width] + turn_sign * with_sine[..., half_width:]
    imag_part = with_cosine[..., half_width:] - turn_sign * with_sine[..., :half_width]
    return jnp.concatenate([real_part, imag_part], -1)


def depth_forward(field_in, tables, factor):
    widened = field_in.astype(jnp.float32)
    with_cosine = jnp.einsum("xycs,sk->kxyc", widened, tables[0], precision=lax.Precision.HIGHEST)
    with_sine = jnp.einsum("xycs,sk->kxyc", widened, tables[1], precision=lax.Precision.HIGHEST)
    return jnp.concatenate([with_cosine, -with_sine], -1) * factor


def depth_inverse(spectra, tables, factor):
    half_width = spectra.shape[-1] // 2
    with_cosine = jnp.einsum(
        "kxyc,sk->xycs", spectra[..., :half_width], tables[0], precision=lax.Precision.HIGHEST
    )
    with_sine = jnp.einsum(
        "kxyc,sk->xycs", spectra[..., half_width:], tables[1], precision=lax.Precision.HIGHEST
    )
    return (with_cosine - with_sine) * factor


def contract_in(left, right):
    return jnp.einsum("mkc,mkco->mko", left, right, precision=lax.Precision.HIGHEST)


def contract_out(left, right):
    return jnp.einsum("mko,mkco->mkc", left, right, precision=lax.Precision.HIGHEST)


def partial_outer(left, right):
    return jnp.einsum("mkc,mko->mkco", left, right, precision=lax.Precision.HIGHEST)


def mix_modes(spectra, weight):
    half_width = spectra.shape[-1] // 2
    weight_wide = weight.astype(jnp.float32)
    weight_real, weight_imag = (weight_wide[..., :half_width], weight_wide[..., half_width:])
    real_in, imag_in = (spectra[..., :half_width], spectra[..., half_width:])
    real_out = contract_in(real_in, weight_real) - contract_in(imag_in, weight_imag)
    imag_out = contract_in(real_in, weight_imag) + contract_in(imag_in, weight_real)
    return jnp.concatenate([real_out, imag_out], -1)


def adjoint_modes(spectra, weight):
    half_width = spectra.shape[-1] // 2
    weight_wide = weight.astype(jnp.float32)
    weight_real, weight_imag = (weight_wide[..., :half_width], weight_wide[..., half_width:])
    real_in, imag_in = (spectra[..., :half_width], spectra[..., half_width:])
    real_out = contract_out(real_in, weight_real) + contract_out(imag_in, weight_imag)
    imag_out = contract_out(imag_in, weight_real) - contract_out(real_in, weight_imag)
    return jnp.concatenate([real_out, imag_out], -1)


def weight_grad(spectra_in, spectra_back):
    half_width = spectra_in.shape[-1] // 2
    real_in, imag_in = (spectra_in[..., :half_width], spectra_in[..., half_width:])
    real_back, imag_back = (spectra_back[..., :half_width], spectra_back[..., half_width:])
    real_part = partial_outer(real_in, real_back) + partial_outer(imag_in, imag_back)
    imag_part = partial_outer(real_in, imag_back) - partial_outer(imag_in, real_back)
    return jnp.concatenate([real_part, imag_part], -1)


def exact_gelu(values):
    return jax.nn.gelu(values, approximate=False)


def per_device(inputs, cotangent, point_weight, spectral_weight):
    rows_x, rows_y, channels, cells = inputs.shape
    mode_rows, mode_cols, flat_width = spectral_weight.shape
    weight_blocks = spectral_weight.reshape(mode_rows, mode_cols, channels, 2 * channels)
    count_gx = lax.axis_size("gx")
    count_gy = lax.axis_size("gy")
    length_x = rows_x * count_gx
    length_y = rows_y * count_gy
    depth_pair = depth_tables()
    own_x = lax.axis_index("gx") * rows_x + jnp.arange(rows_x, dtype=jnp.int32)
    local_x = axis_tables(own_x, KX, length_x)
    whole_y = axis_tables(jnp.arange(length_y, dtype=jnp.int32), KY, length_y)
    total_cells = length_x * length_y * cells
    kept_total = KX * KY * KZ * KT

    def to_modes(field_in, factor):
        depth_spec = settle(depth_forward(field_in, depth_pair, factor))
        share = depth_spec.shape[0] // count_gx
        first_spectra = lax.psum_scatter(
            rotate(
                depth_spec.astype(jnp.float32), local_x[0], local_x[1], "rxyc,xk->rkyc", 1.0
            ).astype(jnp.bfloat16),
            "gx",
            scatter_dimension=0,
            tiled=True,
        ).astype(jnp.float32)
        first_spectra = settle(first_spectra).reshape(share * KX, rows_y, 2 * channels)
        arrived_modes = lax.all_to_all(first_spectra, "gy", split_axis=0, concat_axis=1, tiled=True)
        return rotate(arrived_modes.astype(jnp.float32), whole_y[0], whole_y[1], "myc,yk->mkc", 1.0)

    def to_space(spectra, factor):
        back_rows = settle(rotate(spectra, whole_y[0], whole_y[1], "mkc,yk->myc", -1.0))
        returned = lax.all_to_all(back_rows, "gy", split_axis=1, concat_axis=0, tiled=True)
        share = returned.shape[0] // KX
        returned = returned.reshape(share, KX, rows_y, 2 * channels)
        back_depth = settle(
            rotate(
                lax.all_gather(returned, "gx", axis=0, tiled=True).astype(jnp.float32),
                local_x[0],
                local_x[1],
                "rkyc,xk->rxyc",
                -1.0,
            )
        )
        return depth_inverse(back_depth.astype(jnp.float32), depth_pair, factor)

    spectra_in = to_modes(inputs, 1.0 / math.sqrt(total_cells))
    mixed = mix_modes(spectra_in, weight_blocks)
    spectral_out = to_space(mixed, 1.0 / math.sqrt(kept_total))
    pointwise = jnp.einsum(
        "xycs,co->xyos", inputs, point_weight, preferred_element_type=jnp.float32
    )
    before = spectral_out + pointwise
    unused_out, pullback = jax.vjp(exact_gelu, before)
    slope = settle(pullback(cotangent.astype(jnp.float32))[0])
    spectra_back = to_modes(slope, 1.0 / math.sqrt(kept_total))
    grad_spectral = weight_grad(spectra_in, spectra_back).reshape(mode_rows, mode_cols, flat_width)
    adjoint = adjoint_modes(spectra_back, weight_blocks)
    spectral_grad = to_space(adjoint, 1.0 / math.sqrt(total_cells))
    pointwise_grad = jnp.einsum(
        "xyos,co->xycs", slope, point_weight, preferred_element_type=jnp.float32
    )
    grad_input = (pointwise_grad + spectral_grad).astype(jnp.bfloat16)
    return (grad_input, grad_spectral)


def solution(mesh):
    placed = (
        P("gx", "gy", None, None),
        P("gx", "gy", None, None),
        P(),
        P(("gx", "gy"), None, None),
    )
    return jax.shard_map(
        per_device,
        mesh=mesh,
        in_specs=placed,
        out_specs=(P("gx", "gy", None, None), P(("gx", "gy"), None, None)),
        check_vma=False,
    )
```

profile of v0, /device:TPU:0, one launch (start us, length us, event | category | flops | bytes accessed | tf_op | source)
XLA Modules:
  0.0 453.6 jit_solution(6818993007358127799)
XLA Ops:
  7.4 12.3 %add_sine_fusion = (f32[64,8,12,8]{1,0,3,2:T(8,128)}, f32[64,8,12,8]{1,0,3,2:T(8,128)S(1)}) fusion(f32[8,8]{0,1:T(8,128)S(1)} %fusion.94, f32[64,12]{0,1:T(8,128)S(1)} %fusion.75), kind=kLoop, calls=%fused_computation.19 | loop fusion | flops 49152 | bytes 396544 | tf_op jit(solution)/shard_map/sin | solution.py:33
  19.8 3.9 reshape.129
  23.7 2.8 reshape.128
  31.4 1.6 copy.73
  33.1 31.4 %reduce-scatter.3.cloned.1.call-done = bf16[24,24,2,64]{3,1,2,0:T(8,128)(2,1)} async-done(((bf16[96,24,2,64]{3,1,2,0:T(8,128)(2,1)}), bf16[24,24,2,64]{3,1,2,0:T(8,128)(2,1)}) %reduce-scatter.3.cloned.1.call-update) | async-done | bytes 147472 | tf_op jit(solution)/shard_map/reduce_scatter | solution.py:130
  66.7 4.6 %all-to-all-start = ((bf16[8,2,4608]{2,1,0:T(2,128)(2,1)}), bf16[8,2,4608]{2,1,0:T(2,128)(2,1)S(1)}, u32[]{:S(2)}, u32[]{:S(2)}) async-start(bf16[8,2,4608]{2,1,0:T(2,128)(2,1)} %reshape.154), calls=%async_computation.1 | async-start | bytes 294912 | tf_op jit(solution)/shard_map/all_to_all | solution.py:139
  71.8 20.8 %reshape.123 = bf16[72,24,32,64]{3,2,1,0:T(8,128)(2,1)} reshape(bf16[72,24,2048]{2,1,0:T(8,128)(2,1)} %param.7) | data formatting | bytes 14155776 | tf_op jit(solution)/shard_map/reshape | solution.py:115
  95.3 34.3 %fusion.2 = (f32[72,24,32]{2,1,0:T(8,128)}, f32[72,24,32]{2,1,0:T(8,128)}, f32[72,24,32]{2,1,0:T(8,128)}, f32[72,24,32]{2,1,0:T(8,128)S(1)}) fusion(f32[72,24,32]{2,1,0:T(8,128)S(1)} %copy.146, bf16[72,24,32,64]{3,2,1,0:T(8,128)(2,1)} %reshape.123, f32[72,24,32]{2,1,0:T(8,128)S(1)} %copy.145), kind=kLoop, calls=%fused_computation.10 | loop fusion | flops 17473536 | bytes 8404992
  129.7 2.3 copy.111
  131.9 2.2 copy.119
  134.1 2.2 copy.115
  141.1 14.6 %all_to_all.66 = bf16[72,16,64]{0,2,1:T(8,128)(2,1)S(1)} all-to-all(bf16[72,16,64]{0,2,1:T(8,128)(2,1)S(1)} %copy.78), channel_id=1, replica_groups=mesh['gx'=4,'gy'=8] {'gy'}, dimensions={1} | all-to-all | bytes 294912 | tf_op jit(solution)/shard_map/all_to_all | solution.py:144
  158.0 38.1 %all_gather.6 = bf16[96,24,2,64]{1,0,3,2:T(8,128)(2,1)S(1)} all-gather(bf16[24,24,2,64]{1,0,3,2:T(8,128)(2,1)S(1)} %copy.80), channel_id=1, replica_groups=mesh['gx'=4,'gy'=8] {'gx'}, dimensions={0}, use_global_device_ids=true | all-gather | bytes 737280 | tf_op jit(solution)/shard_map/all_gather | solution.py:149
  196.1 5.8 %convolution_bitcast_fusion.16 = f32[96,4,2,64]{0,1,3,2:T(4,128)S(1)} fusion(bf16[96,24,2,64]{1,0,3,2:T(8,128)(2,1)S(1)} %all_gather.6, s32[24]{0:T(128)S(1)} %compare_select_fusion.2, s32[4]{0:T(128)S(1)} %iota_add_fusion), kind=kOutput, calls=%fused_computation.44 | convolution fusion | flops 14157120 | bytes 786544 | tf_op jit(solution)/shard_map/rkyc,xk->rxyc/dot_general | solution.py:43
  201.9 5.8 %convolution_bitcast_fusion.17 = f32[96,4,2,64]{0,1,3,2:T(4,128)S(1)} fusion(bf16[96,24,2,64]{1,0,3,2:T(8,128)(2,1)S(1)} %all_gather.6, s32[24]{0:T(128)S(1)} %compare_select_fusion.2, s32[4]{0:T(128)S(1)} %iota_add_fusion), kind=kOutput, calls=%fused_computation.45 | convolution fusion | flops 14157120 | bytes 786544 | tf_op jit(solution)/shard_map/rkyc,xk->rxyc/dot_general | solution.py:42
  208.9 2.4 fusion.22
  214.4 1.7 copy.86
  216.1 27.9 %reduce-scatter.5.cloned.1.call-done = bf16[24,24,2,64]{3,1,2,0:T(8,128)(2,1)} async-done(((bf16[96,24,2,64]{3,1,2,0:T(8,128)(2,1)}), bf16[24,24,2,64]{3,1,2,0:T(8,128)(2,1)}) %reduce-scatter.5.cloned.1.call-update) | async-done | bytes 147472 | tf_op jit(solution)/shard_map/reduce_scatter | solution.py:130
  245.5 11.6 %all_to_all.67 = bf16[8,2,4608]{2,1,0:T(2,128)(2,1)S(1)} all-to-all(bf16[8,2,4608]{2,1,0:T(2,128)(2,1)S(1)} %reshape.156), channel_id=1, replica_groups=mesh['gx'=4,'gy'=8] {'gy'}, dimensions={0} | all-to-all | bytes 294912 | tf_op jit(solution)/shard_map/all_to_all | solution.py:139
  261.3 2.3 copy.148
  263.6 38.7 %fusion.6 = (f32[72,24,32]{2,1,0:T(8,128)}, f32[72,24,32]{2,1,0:T(8,128)}, f32[72,24,32]{2,1,0:T(8,128)}, f32[72,24,32]{2,1,0:T(8,128)}) fusion(f32[72,24,32]{2,1,0:T(8,128)} %copy.148, bf16[72,24,32,64]{3,2,1,0:T(8,128)(2,1)} %reshape.123, f32[72,24,32]{2,1,0:T(8,128)S(1)} %copy.147), kind=kLoop, calls=%fused_computation.14 | loop fusion | flops 17473536 | bytes 8404992
  302.3 2.2 copy.131
  304.4 2.2 copy.136
  306.6 2.2 copy.141
  308.8 2.2 copy.126
  314.6 20.0 %multiply_add_fusion = (f32[72,24,32,32]{3,2,1,0:T(8,128)}, f32[72,24,32,32]{3,2,1,0:T(8,128)}) fusion(f32[72,24,32]{2,1,0:T(8,128)S(1)} %copy.146, f32[72,24,32]{2,1,0:T(8,128)S(1)} %copy.145, f32[72,24,32]{2,1,0:T(8,128)} %copy.148, f32[72,24,32]{2,1,0:T(8,128)S(1)} %copy.147), kind=kLoop, calls=%fused_computation.18 | loop fusion | flops 10616832 | bytes 15040512 | tf_op jit(solution)/shard_map/add | solution.py:103
  335.5 3.7 all-to-all-start.3
  339.2 28.5 %pad_maximum_fusion = f32[72,24,32,64]{3,2,1,0:T(8,128)} fusion(f32[72,24,32,32]{3,2,1,0:T(8,128)} %get-tuple-element.15, f32[72,24,32,32]{3,2,1,0:T(8,128)} %get-tuple-element.14), kind=kLoop, calls=%fused_computation.16 | loop fusion | flops 3538944 | bytes 28311552 | tf_op jit(solution)/shard_map/concatenate | solution.py:105
  367.7 24.3 %reshape.127 = f32[72,24,2048]{2,1,0:T(8,128)} reshape(f32[72,24,32,64]{3,2,1,0:T(8,128)} %pad_maximum_fusion) | data formatting | bytes 28311552 | tf_op jit(solution)/shard_map/reshape | solution.py:168
  392.7 40.0 %all_gather.7 = bf16[96,24,2,64]{1,0,3,2:T(8,128)(2,1)S(1)} all-gather(bf16[24,24,2,64]{1,0,3,2:T(8,128)(2,1)S(1)} %copy.93), channel_id=1, replica_groups=mesh['gx'=4,'gy'=8] {'gx'}, dimensions={0}, use_global_device_ids=true | all-gather | bytes 737280 | tf_op jit(solution)/shard_map/all_gather | solution.py:149
  432.7 5.8 %convolution_bitcast_fusion.14 = f32[96,4,2,64]{0,1,3,2:T(4,128)S(1)} fusion(bf16[96,24,2,64]{1,0,3,2:T(8,128)(2,1)S(1)} %all_gather.7, s32[24]{0:T(128)S(1)} %compare_select_fusion.2, s32[4]{0:T(128)S(1)} %iota_add_fusion), kind=kOutput, calls=%fused_computation.42 | convolution fusion | flops 14157120 | bytes 786544 | tf_op jit(solution)/shard_map/rkyc,xk->rxyc/dot_general | solution.py:43
  438.5 5.8 %convolution_bitcast_fusion.15 = f32[96,4,2,64]{0,1,3,2:T(4,128)S(1)} fusion(bf16[96,24,2,64]{1,0,3,2:T(8,128)(2,1)S(1)} %all_gather.7, s32[24]{0:T(128)S(1)} %compare_select_fusion.2, s32[4]{0:T(128)S(1)} %iota_add_fusion), kind=kOutput, calls=%fused_computation.43 | convolution fusion | flops 14157120 | bytes 786544 | tf_op jit(solution)/shard_map/rkyc,xk->rxyc/dot_general | solution.py:42
  (91 shorter events, 34.3 us)
Async XLA Ops:
  7.2 19.3 %copy-start = (bf16[4,2,32,512]{3,2,1,0:T(8,128)(2,1)S(1)}, bf16[4,2,32,512]{3,2,1,0:T(8,128)(2,1)}, u32[]{:S(2)}) copy-start(bf16[4,2,32,512]{3,2,1,0:T(8,128)(2,1)} %param.4) | copy-start | bytes 786436
  7.2 57.3 %reduce-scatter.3.cloned.1.call-start = ((), (), s32[]{:S(2)}) async-start(), calls=%async_computation.6 | async-start | bytes 1474560 | tf_op jit(solution)/shard_map/reduce_scatter | solution.py:130
  66.7 26.0 %all-to-all-start = ((bf16[8,2,4608]{2,1,0:T(2,128)(2,1)}), bf16[8,2,4608]{2,1,0:T(2,128)(2,1)S(1)}, u32[]{:S(2)}, u32[]{:S(2)}) async-start(bf16[8,2,4608]{2,1,0:T(2,128)(2,1)} %reshape.154), calls=%async_computation.1 | async-start | bytes 294912 | tf_op jit(solution)/shard_map/all_to_all | solution.py:139
  71.3 172.7 %reduce-scatter.5.cloned.1.call-start = ((), (), s32[]{:S(2)}) async-start(), calls=%async_computation.7 | async-start | bytes 1474560 | tf_op jit(solution)/shard_map/reduce_scatter | solution.py:130
  129.6 78.4 %copy-start.3 = (f32[512,96,1,1]{0,1,2,3:T(8,128)S(1)}, f32[512,96,1,1]{0,1,2,3:T(8,128)}, u32[]{:S(2)}) copy-start(f32[512,96,1,1]{0,1,2,3:T(8,128)} %reshape.128) | copy-start | bytes 589828
  129.7 78.8 %copy-start.2 = (f32[512,96,1,1]{0,1,2,3:T(8,128)S(1)}, f32[512,96,1,1]{0,1,2,3:T(8,128)}, u32[]{:S(2)}) copy-start(f32[512,96,1,1]{0,1,2,3:T(8,128)} %reshape.129) | copy-start | bytes 589828
  129.7 79.2 %copy-start.6 = (bf16[32,32]{1,0:T(8,128)(2,1)S(1)}, bf16[32,32]{1,0:T(8,128)(2,1)}, u32[]{:S(2)}) copy-start(bf16[32,32]{1,0:T(8,128)(2,1)} %param.6) | copy-start | bytes 6148
  211.2 3.0 copy-start.4
  335.5 56.5 %all-to-all-start.3 = ((bf16[72,16,64]{0,2,1:T(8,128)(2,1)}), bf16[72,16,64]{0,2,1:T(8,128)(2,1)S(1)}, u32[]{:S(2)}, u32[]{:S(2)}) async-start(bf16[72,16,64]{0,2,1:T(8,128)(2,1)} %copy.91), calls=%async_computation.5 | async-start | bytes 524288 | tf_op jit(solution)/shard_map/all_to_all | solution.py:144
  367.7 78.6 %copy-start.1 = (bf16[4,2,32,512]{3,2,1,0:T(8,128)(2,1)S(1)}, bf16[4,2,32,512]{3,2,1,0:T(8,128)(2,1)}, u32[]{:S(2)}) copy-start(bf16[4,2,32,512]{3,2,1,0:T(8,128)(2,1)} %param.4) | copy-start | bytes 786436
  392.0 53.4 %copy-start.5 = (bf16[4,2,32,512]{3,2,1,0:T(8,128)(2,1)S(1)}, bf16[4,2,32,512]{3,2,1,0:T(8,128)(2,1)}, u32[]{:S(2)}) copy-start(bf16[4,2,32,512]{3,2,1,0:T(8,128)(2,1)} %copy-done.4) | copy-start | bytes 786436
Sparse Core Ops, SparseCore 0:
  33.2 31.2 reduce-scatter.2
  216.2 27.7 reduce-scatter.4
where the time goes:
time: 463 us; the launch traced here: 454 us
  other arithmetic  141 us (30%)
  blocking collectives  104 us (22%)
  local copies, waits for them, and re-layouts  84.9 us (18%)
  waiting for transfers between devices  59.4 us (13%)
  matrix products  40.2 us (9%)
  between operations  15 us (3%)
  starting transfers between devices  8.86 us (2%)
    all_gather x2, blocking collectives, to_space(): lax.all_gather(returned, 'gx', axis=0, tiled=True).astype(jnp.float32)  78.1 us
    unnamed x2, other arithmetic  73 us
    reduce_scatter x2, waiting for transfers between devices, to_modes(): lax.psum_scatter(rotate(depth_spec.astype(jnp.float32), local_x[0], local...  59.3 us
    concatenate x1, other arithmetic, weight_grad(): return jnp.concatenate([real_part, imag_part], -1)  28.5 us
    reshape x1, local copies, waits for them, and re-layouts, per_device(): weight_grad(spectra_in, spectra_back)  24.3 us
    reshape x1, local copies, waits for them, and re-layouts, per_device(): spectral_weight.reshape(mode_rows, mode_cols, channels, 2 * channels)  20.8 us
    add x1, other arithmetic, weight_grad(): partial_outer(real_in, real_back) + partial_outer(imag_in, imag_back)  20 us
    dot_general x8, matrix products, rotate(): jnp.einsum(pattern, spectra, cosine_table, precision=lax.Precision.HIGHEST)  16 us
  transfers between devices with their start and end apart: 4, of which 2 were waited for; matrix products, arithmetic and copies ran while one was open for 16% of the time, Pallas kernels for 0%

commit v1 on v0

--- a/solution.py
+++ b/solution.py
@@ -10,6 +10,17 @@
 KY = 24
 KZ = 12
 KT = 8
+
+
+def in_blocks(value, dim, size):
+    before, after = (value.shape[:dim], value.shape[dim + 1 :])
+    return jnp.moveaxis(value.reshape(*before, size, -1, *after), dim, 0)
+
+
+def laid_out(blocks, dim):
+    blocks = jnp.moveaxis(blocks, 0, dim)
+    lengths = blocks.shape
+    return blocks.reshape(*lengths[:dim], lengths[dim] * lengths[dim + 1], *lengths[dim + 2 :])
 
 
 def kept_angles(positions, kept_count, length):
@@ -141,7 +152,14 @@
 
     def to_space(spectra, factor):
         back_rows = settle(rotate(spectra, whole_y[0], whole_y[1], "mkc,yk->myc", -1.0))
-        returned = lax.all_to_all(back_rows, "gy", split_axis=1, concat_axis=0, tiled=True)
+        size, here = (lax.axis_size("gy"), lax.axis_index("gy"))
+        blocks = in_blocks(back_rows, 1, size)
+        gathered = [blocks[here]]
+        for step in range(1, size):
+            sent = blocks[(here + step) % size]
+            gathered.append(lax.ppermute(sent, "gy", [(i, (i + step) % size) for i in range(size)]))
+        blocks = jnp.stack(gathered)[(here - jnp.arange(size)) % size]
+        returned = laid_out(blocks, 0)
         share = returned.shape[0] // KX
         returned = returned.reshape(share, KX, rows_y, 2 * channels)
         back_depth = settle(

time: 463 us -> 464 us (level)
  starting transfers between devices: 8.86 us -> 22.3 us
  blocking collectives: 104 us -> 93.2 us
  other arithmetic: 141 us -> 135 us
    ppermute x0 -> x14, starting transfers between devices: none -> 17.5 us  [to_space(): lax.ppermute(sent, 'gy', [(i, (i + step) % size) for i in range(size)])]
    all_to_all x1 -> x0, blocking collectives: 14.6 us -> none  [to_space(): lax.all_to_all(back_rows, 'gy', split_axis=1, concat_axis=0, tiled=True)]
    concatenate x1, other arithmetic: 28.5 us -> 22.3 us  [weight_grad(): return jnp.concatenate([real_part, imag_part], -1)]
  transfers between devices with their start and end apart: 4 -> 17, of which waited for: 2 -> 7; matrix products, arithmetic and copies ran while one was open for 16% -> 15% of each run, Pallas kernels for 0% -> 0%
where the time goes in v1:
time: 464 us; the launch traced here: 455 us
  other arithmetic  135 us (29%)
  blocking collectives  93.2 us (20%)
  local copies, waits for them, and re-layouts  86 us (19%)
  waiting for transfers between devices  63 us (14%)
  matrix products  40.2 us (9%)
  starting transfers between devices  22.3 us (5%)
  between operations  15.1 us (3%)
    all_gather x2, blocking collectives, to_space(): lax.all_gather(returned, 'gx', axis=0, tiled=True).astype(jnp.float32)  81.4 us
    unnamed x2, other arithmetic  73 us
    reduce_scatter x2, waiting for transfers between devices, to_modes(): lax.psum_scatter(rotate(depth_spec.astype(jnp.float32), local_x[0], local...  59.9 us
    reshape x1, local copies, waits for them, and re-layouts, per_device(): weight_grad(spectra_in, spectra_back)  24.3 us
    concatenate x1, other arithmetic, weight_grad(): return jnp.concatenate([real_part, imag_part], -1)  22.3 us
    reshape x1, local copies, waits for them, and re-layouts, per_device(): spectral_weight.reshape(mode_rows, mode_cols, channels, 2 * channels)  20.8 us
    add x1, other arithmetic, weight_grad(): partial_outer(real_in, real_back) + partial_outer(imag_in, imag_back)  20.4 us
    ppermute x14, starting transfers between devices, to_space(): lax.ppermute(sent, 'gy', [(i, (i + step) % size) for i in range(size)])  17.5 us
  transfers between devices with their start and end apart: 17, of which 7 were waited for; matrix products, arithmetic and copies ran while one was open for 15% of the time, Pallas kernels for 0%

profile of v1, /device:TPU:0, one launch (start us, length us, event | category | flops | bytes accessed | tf_op | source)
XLA Modules:
  0.0 455.1 jit_solution(13285788758404191739)
XLA Ops:
  7.4 12.3 %add_sine_fusion = (f32[64,8,12,8]{1,0,3,2:T(8,128)}, f32[64,8,12,8]{1,0,3,2:T(8,128)S(1)}) fusion(f32[8,8]{0,1:T(8,128)S(1)} %fusion.94, f32[64,12]{0,1:T(8,128)S(1)} %fusion.75), kind=kLoop, calls=%fused_computation.21 | loop fusion | flops 49152 | bytes 396544 | tf_op jit(solution)/shard_map/sin | solution.py:44
  19.8 3.9 reshape.222
  23.7 2.8 reshape.221
  33.1 31.4 %reduce-scatter.3.cloned.1.call-done = bf16[24,24,2,64]{3,1,2,0:T(8,128)(2,1)} async-done(((bf16[96,24,2,64]{3,1,2,0:T(8,128)(2,1)}), bf16[24,24,2,64]{3,1,2,0:T(8,128)(2,1)}) %reduce-scatter.3.cloned.1.call-update) | async-done | bytes 147472 | tf_op jit(solution)/shard_map/reduce_scatter | solution.py:141
  66.7 4.6 %all-to-all-start = ((bf16[8,2,4608]{2,1,0:T(2,128)(2,1)}), bf16[8,2,4608]{2,1,0:T(2,128)(2,1)S(1)}, u32[]{:S(2)}, u32[]{:S(2)}) async-start(bf16[8,2,4608]{2,1,0:T(2,128)(2,1)} %reshape.247), calls=%async_computation.1 | async-start | bytes 294912 | tf_op jit(solution)/shard_map/all_to_all | solution.py:150
  71.6 20.8 %reshape.200 = bf16[72,24,32,64]{3,2,1,0:T(8,128)(2,1)} reshape(bf16[72,24,2048]{2,1,0:T(8,128)(2,1)} %param.7) | data formatting | bytes 14155776 | tf_op jit(solution)/shard_map/reshape | solution.py:126
  95.1 34.4 %fusion.2 = (f32[72,24,32]{2,1,0:T(8,128)}, f32[72,24,32]{2,1,0:T(8,128)}, f32[72,24,32]{2,1,0:T(8,128)}, f32[72,24,32]{2,1,0:T(8,128)S(1)}) fusion(f32[72,24,32]{2,1,0:T(8,128)S(1)} %copy.147, bf16[72,24,32,64]{3,2,1,0:T(8,128)(2,1)} %reshape.200, f32[72,24,32]{2,1,0:T(8,128)S(1)} %copy.146), kind=kLoop, calls=%fused_computation.12 | loop fusion | flops 17473536 | bytes 8404992
  129.5 2.3 copy.112
  131.8 2.3 copy.120
  134.0 2.2 copy.116
  141.8 1.7 collective-permute-start.1
  143.5 2.2 collective-permute-start.2
  155.6 40.6 %all_gather.6 = bf16[96,24,2,64]{1,0,3,2:T(8,128)(2,1)S(1)} all-gather(bf16[24,24,2,64]{1,0,3,2:T(8,128)(2,1)S(1)} %copy.74), channel_id=1, replica_groups=mesh['gx'=4,'gy'=8] {'gx'}, dimensions={0}, use_global_device_ids=true | all-gather | bytes 737280 | tf_op jit(solution)/shard_map/all_gather | solution.py:167
  196.2 5.8 %convolution_bitcast_fusion.16 = f32[96,4,2,64]{0,1,3,2:T(4,128)S(1)} fusion(bf16[96,24,2,64]{1,0,3,2:T(8,128)(2,1)S(1)} %all_gather.6, s32[24]{0:T(128)S(1)} %compare_select_fusion.3, s32[4]{0:T(128)S(1)} %iota_add_fusion), kind=kOutput, calls=%fused_computation.46 | convolution fusion | flops 14157120 | bytes 786544 | tf_op jit(solution)/shard_map/rkyc,xk->rxyc/dot_general | solution.py:54
  202.0 5.8 %convolution_bitcast_fusion.17 = f32[96,4,2,64]{0,1,3,2:T(4,128)S(1)} fusion(bf16[96,24,2,64]{1,0,3,2:T(8,128)(2,1)S(1)} %all_gather.6, s32[24]{0:T(128)S(1)} %compare_select_fusion.3, s32[4]{0:T(128)S(1)} %iota_add_fusion), kind=kOutput, calls=%fused_computation.47 | convolution fusion | flops 14157120 | bytes 786544 | tf_op jit(solution)/shard_map/rkyc,xk->rxyc/dot_general | solution.py:53
  209.0 2.4 fusion.22
  216.2 28.5 %reduce-scatter.5.cloned.1.call-done = bf16[24,24,2,64]{3,1,2,0:T(8,128)(2,1)} async-done(((bf16[96,24,2,64]{3,1,2,0:T(8,128)(2,1)}), bf16[24,24,2,64]{3,1,2,0:T(8,128)(2,1)}) %reduce-scatter.5.cloned.1.call-update) | async-done | bytes 147472 | tf_op jit(solution)/shard_map/reduce_scatter | solution.py:141
  246.2 11.8 %all_to_all.36 = bf16[8,2,4608]{2,1,0:T(2,128)(2,1)S(1)} all-to-all(bf16[8,2,4608]{2,1,0:T(2,128)(2,1)S(1)} %reshape.249), channel_id=1, replica_groups=mesh['gx'=4,'gy'=8] {'gy'}, dimensions={0} | all-to-all | bytes 294912 | tf_op jit(solution)/shard_map/all_to_all | solution.py:150
  262.2 2.3 copy.149
  264.4 38.6 %fusion.6 = (f32[72,24,32]{2,1,0:T(8,128)}, f32[72,24,32]{2,1,0:T(8,128)}, f32[72,24,32]{2,1,0:T(8,128)}, f32[72,24,32]{2,1,0:T(8,128)}) fusion(f32[72,24,32]{2,1,0:T(8,128)} %copy.149, bf16[72,24,32,64]{3,2,1,0:T(8,128)(2,1)} %reshape.200, f32[72,24,32]{2,1,0:T(8,128)S(1)} %copy.148), kind=kLoop, calls=%fused_computation.16 | loop fusion | flops 17473536 | bytes 8404992
  303.0 2.2 copy.132
  305.2 2.2 copy.137
  307.4 2.2 copy.142
  309.7 2.2 copy.127
  315.5 20.4 %multiply_add_fusion = (f32[72,24,32,32]{3,2,1,0:T(8,128)S(1)}, f32[72,24,32,32]{3,2,1,0:T(8,128)}) fusion(f32[72,24,32]{2,1,0:T(8,128)S(1)} %copy.147, f32[72,24,32]{2,1,0:T(8,128)S(1)} %copy.146, f32[72,24,32]{2,1,0:T(8,128)} %copy.149, f32[72,24,32]{2,1,0:T(8,128)S(1)} %copy.148), kind=kLoop, calls=%fused_computation.20 | loop fusion | flops 10616832 | bytes 15040512 | tf_op jit(solution)/shard_map/add | solution.py:114
  338.5 2.7 collective-permute-start.10
  341.3 22.3 %pad_maximum_fusion = f32[72,24,32,64]{3,2,1,0:T(8,128)} fusion(f32[72,24,32,32]{3,2,1,0:T(8,128)} %get-tuple-element.15, f32[72,24,32,32]{3,2,1,0:T(8,128)S(1)} %get-tuple-element.14), kind=kLoop, calls=%fused_computation.18 | loop fusion | flops 3538944 | bytes 28311552 | tf_op jit(solution)/shard_map/concatenate | solution.py:116
  363.7 24.3 %reshape.204 = f32[72,24,2048]{2,1,0:T(8,128)} reshape(f32[72,24,32,64]{3,2,1,0:T(8,128)} %pad_maximum_fusion) | data formatting | bytes 28311552 | tf_op jit(solution)/shard_map/reshape | solution.py:186
  388.0 2.1 collective-permute-start.12
  393.6 40.8 %all_gather.7 = bf16[96,24,2,64]{1,0,3,2:T(8,128)(2,1)S(1)} all-gather(bf16[24,24,2,64]{1,0,3,2:T(8,128)(2,1)S(1)} %copy.94), channel_id=1, replica_groups=mesh['gx'=4,'gy'=8] {'gx'}, dimensions={0}, use_global_device_ids=true | all-gather | bytes 737280 | tf_op jit(solution)/shard_map/all_gather | solution.py:167
  434.4 5.8 %convolution_bitcast_fusion.14 = f32[96,4,2,64]{0,1,3,2:T(4,128)S(1)} fusion(bf16[96,24,2,64]{1,0,3,2:T(8,128)(2,1)S(1)} %all_gather.7, s32[24]{0:T(128)S(1)} %compare_select_fusion.3, s32[4]{0:T(128)S(1)} %iota_add_fusion), kind=kOutput, calls=%fused_computation.44 | convolution fusion | flops 14157120 | bytes 786544 | tf_op jit(solution)/shard_map/rkyc,xk->rxyc/dot_general | solution.py:54
  440.2 5.8 %convolution_bitcast_fusion.15 = f32[96,4,2,64]{0,1,3,2:T(4,128)S(1)} fusion(bf16[96,24,2,64]{1,0,3,2:T(8,128)(2,1)S(1)} %all_gather.7, s32[24]{0:T(128)S(1)} %compare_select_fusion.3, s32[4]{0:T(128)S(1)} %iota_add_fusion), kind=kOutput, calls=%fused_computation.45 | convolution fusion | flops 14157120 | bytes 786544 | tf_op jit(solution)/shard_map/rkyc,xk->rxyc/dot_general | solution.py:53
  (150 shorter events, 50.2 us)
Async XLA Ops:
  7.2 19.3 %copy-start = (bf16[4,2,32,512]{3,2,1,0:T(8,128)(2,1)S(1)}, bf16[4,2,32,512]{3,2,1,0:T(8,128)(2,1)}, u32[]{:S(2)}) copy-start(bf16[4,2,32,512]{3,2,1,0:T(8,128)(2,1)} %param.4) | copy-start | bytes 786436
  7.2 57.3 %reduce-scatter.3.cloned.1.call-start = ((), (), s32[]{:S(2)}) async-start(), calls=%async_computation.4 | async-start | bytes 1474560 | tf_op jit(solution)/shard_map/reduce_scatter | solution.py:141
  66.7 25.8 %all-to-all-start = ((bf16[8,2,4608]{2,1,0:T(2,128)(2,1)}), bf16[8,2,4608]{2,1,0:T(2,128)(2,1)S(1)}, u32[]{:S(2)}, u32[]{:S(2)}) async-start(bf16[8,2,4608]{2,1,0:T(2,128)(2,1)} %reshape.247), calls=%async_computation.1 | async-start | bytes 294912 | tf_op jit(solution)/shard_map/all_to_all | solution.py:150
  71.3 173.4 %reduce-scatter.5.cloned.1.call-start = ((), (), s32[]{:S(2)}) async-start(), calls=%async_computation.5 | async-start | bytes 1474560 | tf_op jit(solution)/shard_map/reduce_scatter | solution.py:141
  129.5 78.7 %copy-start.3 = (f32[512,96,1,1]{0,1,2,3:T(8,128)S(1)}, f32[512,96,1,1]{0,1,2,3:T(8,128)}, u32[]{:S(2)}) copy-start(f32[512,96,1,1]{0,1,2,3:T(8,128)} %reshape.221) | copy-start | bytes 589828
  129.5 79.1 %copy-start.2 = (f32[512,96,1,1]{0,1,2,3:T(8,128)S(1)}, f32[512,96,1,1]{0,1,2,3:T(8,128)}, u32[]{:S(2)}) copy-start(f32[512,96,1,1]{0,1,2,3:T(8,128)} %reshape.222) | copy-start | bytes 589828
  131.8 77.2 %copy-start.6 = (bf16[32,32]{1,0:T(8,128)(2,1)S(1)}, bf16[32,32]{1,0:T(8,128)(2,1)}, u32[]{:S(2)}) copy-start(bf16[32,32]{1,0:T(8,128)(2,1)} %param.6) | copy-start | bytes 6148
  141.3 6.9 %collective-permute-start = (bf16[72,2,64]{0,2,1:T(8,128)(2,1)S(1)}, bf16[72,2,64]{0,2,1:T(8,128)(2,1)S(1)}, u32[]{:S(2)}, u32[]{:S(2)}) collective-permute-start(bf16[72,2,64]{0,2,1:T(8,128)(2,1)S(1)} %bitcast.257), channel_id=1, source_target_pairs={{0,1},{1,2},{2,3},{3,4},{4,5},{5,6},{6,7},{7,0},{8,9},{9,10},{10,1... | collective-permute-start | bytes 55304 | tf_op jit(solution)/shard_map/ppermute | solution.py:160
  141.8 8.0 %collective-permute-start.1 = (bf16[72,2,64]{0,2,1:T(8,128)(2,1)S(1)}, bf16[72,2,64]{0,2,1:T(8,128)(2,1)S(1)}, u32[]{:S(2)}, u32[]{:S(2)}) collective-permute-start(bf16[72,2,64]{0,2,1:T(8,128)(2,1)S(1)} %bitcast.255), channel_id=1, source_target_pairs={{0,2},{1,3},{2,4},{3,5},{4,6},{5,7},{6,0},{7,1},{8,10},{9,11},{10,... | collective-permute-start | bytes 55304 | tf_op jit(solution)/shard_map/ppermute | solution.py:160
  143.5 7.7 %collective-permute-start.2 = (bf16[72,2,64]{0,2,1:T(8,128)(2,1)S(1)}, bf16[72,2,64]{0,2,1:T(8,128)(2,1)S(1)}, u32[]{:S(2)}, u32[]{:S(2)}) collective-permute-start(bf16[72,2,64]{0,2,1:T(8,128)(2,1)S(1)} %bitcast.250), channel_id=1, source_target_pairs={{0,3},{1,4},{2,5},{3,6},{4,7},{5,0},{6,1},{7,2},{8,11},{9,12},{10,... | collective-permute-start | bytes 55304 | tf_op jit(solution)/shard_map/ppermute | solution.py:160
  145.7 5.5 %collective-permute-start.3 = (bf16[72,2,64]{0,2,1:T(8,128)(2,1)S(1)}, bf16[72,2,64]{0,2,1:T(8,128)(2,1)S(1)}, u32[]{:S(2)}, u32[]{:S(2)}) collective-permute-start(bf16[72,2,64]{0,2,1:T(8,128)(2,1)S(1)} %bitcast.247), channel_id=1, source_target_pairs={{0,4},{1,5},{2,6},{3,7},{4,0},{5,1},{6,2},{7,3},{8,12},{9,13},{10,... | collective-permute-start | bytes 55304 | tf_op jit(solution)/shard_map/ppermute | solution.py:160
  147.1 4.1 collective-permute-start.4
  148.2 4.0 collective-permute-start.5
  149.8 3.0 collective-permute-start.6
  211.4 3.0 copy-start.4
  336.3 51.7 %collective-permute-start.7 = (bf16[72,2,64]{0,2,1:T(8,128)(2,1)S(1)}, bf16[72,2,64]{0,2,1:T(8,128)(2,1)S(1)}, u32[]{:S(2)}, u32[]{:S(2)}) collective-permute-start(bf16[72,2,64]{0,2,1:T(8,128)(2,1)S(1)} %bitcast.256), channel_id=1, source_target_pairs={{0,1},{1,2},{2,3},{3,4},{4,5},{5,6},{6,7},{7,0},{8,9},{9,10},{10,1... | collective-permute-start | bytes 55304 | tf_op jit(solution)/shard_map/ppermute | solution.py:160
  336.4 53.7 %collective-permute-start.8 = (bf16[72,2,64]{0,2,1:T(8,128)(2,1)S(1)}, bf16[72,2,64]{0,2,1:T(8,128)(2,1)S(1)}, u32[]{:S(2)}, u32[]{:S(2)}) collective-permute-start(bf16[72,2,64]{0,2,1:T(8,128)(2,1)S(1)} %bitcast.252), channel_id=1, source_target_pairs={{0,2},{1,3},{2,4},{3,5},{4,6},{5,7},{6,0},{7,1},{8,10},{9,11},{10,... | collective-permute-start | bytes 55304 | tf_op jit(solution)/shard_map/ppermute | solution.py:160
  337.4 53.3 %collective-permute-start.9 = (bf16[72,2,64]{0,2,1:T(8,128)(2,1)S(1)}, bf16[72,2,64]{0,2,1:T(8,128)(2,1)S(1)}, u32[]{:S(2)}, u32[]{:S(2)}) collective-permute-start(bf16[72,2,64]{0,2,1:T(8,128)(2,1)S(1)} %bitcast.248), channel_id=1, source_target_pairs={{0,3},{1,4},{2,5},{3,6},{4,7},{5,0},{6,1},{7,2},{8,11},{9,12},{10,... | collective-permute-start | bytes 55304 | tf_op jit(solution)/shard_map/ppermute | solution.py:160
  338.5 52.3 %collective-permute-start.10 = (bf16[72,2,64]{0,2,1:T(8,128)(2,1)S(1)}, bf16[72,2,64]{0,2,1:T(8,128)(2,1)S(1)}, u32[]{:S(2)}, u32[]{:S(2)}) collective-permute-start(bf16[72,2,64]{0,2,1:T(8,128)(2,1)S(1)} %bitcast.246), channel_id=1, source_target_pairs={{0,4},{1,5},{2,6},{3,7},{4,0},{5,1},{6,2},{7,3},{8,12},{9,13},{10,... | collective-permute-start | bytes 55304 | tf_op jit(solution)/shard_map/ppermute | solution.py:160
  341.2 49.6 %collective-permute-start.11 = (bf16[72,2,64]{0,2,1:T(8,128)(2,1)S(1)}, bf16[72,2,64]{0,2,1:T(8,128)(2,1)S(1)}, u32[]{:S(2)}, u32[]{:S(2)}) collective-permute-start(bf16[72,2,64]{0,2,1:T(8,128)(2,1)S(1)} %bitcast.244), channel_id=1, source_target_pairs={{0,5},{1,6},{2,7},{3,0},{4,1},{5,2},{6,3},{7,4},{8,13},{9,14},{10,... | collective-permute-start | bytes 55304 | tf_op jit(solution)/shard_map/ppermute | solution.py:160
  363.7 84.4 %copy-start.1 = (bf16[4,2,32,512]{3,2,1,0:T(8,128)(2,1)S(1)}, bf16[4,2,32,512]{3,2,1,0:T(8,128)(2,1)}, u32[]{:S(2)}) copy-start(bf16[4,2,32,512]{3,2,1,0:T(8,128)(2,1)} %param.4) | copy-start | bytes 786436
  388.0 59.1 %copy-start.5 = (bf16[4,2,32,512]{3,2,1,0:T(8,128)(2,1)S(1)}, bf16[4,2,32,512]{3,2,1,0:T(8,128)(2,1)}, u32[]{:S(2)}) copy-start(bf16[4,2,32,512]{3,2,1,0:T(8,128)(2,1)} %copy-done.4) | copy-start | bytes 786436
  388.0 3.9 collective-permute-start.12
  390.1 2.2 collective-permute-start.13
Sparse Core Ops, SparseCore 0:
  33.2 31.2 reduce-scatter.2
  216.3 28.3 reduce-scatter.4
